TPU v7x, 128 devices: a whole 4x4x4 slice. The times are simulated.
128 devices in a mesh: pair: 2 (over core), batch: 4 (over y), vocab: 16 (over x, z).
Axes of the slice: x: 4, y: 4, z: 4, core: 2. Of those that a mesh axis runs over, the one named last changes fastest.
Arguments:
- hidden: bfloat16 [2, 512, 8192], P('pair', 'batch', 'vocab'), may hold values from -120 to 120
- norm_gain: bfloat16 [8192], P('vocab'), may hold values from 0.099609375 to 1.8984375
- head_weight: bfloat16 [8192, 65536], P(('pair', 'batch'), 'vocab'), may hold values from -1 to 1
Outputs:
- guided_logprobs: float32 [512, 65536], P(('pair', 'batch'), 'vocab')
- cond_logprobs: float32 [512, 65536], P(('pair', 'batch'), 'vocab')
All inputs are finite; a program needn't handle non-finite values.
Results may differ from a plain program's by a relative error of at most 0.007.
Values may be sent and summed in bfloat16 or wider, within the bound.
A program may use at most 128 MiB of HBM per device.

v0:
```python
import jax
import jax.numpy as jnp
from jax import lax
from jax.sharding import PartitionSpec as P

D = 8192
EPS = 1e-05
GUIDE = 1.5


def on_device(hidden, norm_gain, head_weight):
    rows = lax.all_gather(hidden[0], "vocab", axis=1, tiled=True)
    gain = lax.all_gather(norm_gain, "vocab", axis=0, tiled=True)
    wide = rows.astype(jnp.float32)
    total_sq = jnp.sum(wide * wide, axis=1)
    scaled = wide * lax.rsqrt(total_sq / D + EPS)[:, None] * gain.astype(jnp.float32)[None, :]
    features = scaled.astype(jnp.bfloat16)
    blocks = lax.all_to_all(features, ("pair", "batch"), split_axis=1, concat_axis=0, tiled=True)
    groups = lax.axis_size("pair") * lax.axis_size("batch")
    width = blocks.shape[1]
    out_rows = blocks.shape[0] // (2 * groups)
    ordered = blocks.reshape(2, groups, out_rows, width).transpose(1, 0, 2, 3).reshape(-1, width)
    logits = lax.psum_scatter(
        jnp.dot(ordered, head_weight, preferred_element_type=jnp.float32),
        ("pair", "batch"),
        scatter_dimension=0,
        tiled=True,
    )
    cond = logits[:out_rows]
    uncond = logits[out_rows:]
    guided = GUIDE * cond + (1.0 - GUIDE) * uncond
    peak_c = jnp.max(cond, axis=1)
    peak_g = jnp.max(guided, axis=1)
    local_c = jnp.sum(jnp.exp(cond - peak_c[:, None]), axis=1)
    local_g = jnp.sum(jnp.exp(guided - peak_g[:, None]), axis=1)
    stats = jnp.stack([peak_c, local_c, peak_g, local_g])
    every = lax.all_gather(stats, "vocab", axis=0)
    top_c = jnp.max(every[:, 0], axis=0)
    top_g = jnp.max(every[:, 2], axis=0)
    total_c = jnp.sum(every[:, 1] * jnp.exp(every[:, 0] - top_c[None, :]), axis=0)
    total_g = jnp.sum(every[:, 3] * jnp.exp(every[:, 2] - top_g[None, :]), axis=0)
    cond_out = cond - (top_c + jnp.log(total_c))[:, None]
    guided_out = guided - (top_g + jnp.log(total_g))[:, None]
    return (guided_out, cond_out)


def solution(mesh):
    in_specs = (P("pair", "batch", "vocab"), P("vocab"), P(("pair", "batch"), "vocab"))
    out_specs = (P(("pair", "batch"), "vocab"), P(("pair", "batch"), "vocab"))
    return jax.shard_map(
        on_device, mesh=mesh, in_specs=in_specs, out_specs=out_specs, check_vma=False
    )
```

profile of v0, /device:TPU:0, one launch (start us, length us, event | category | flops | bytes accessed | tf_op | source)
XLA Modules:
  0.0 317.6 jit_solution(5014193301131208361)
XLA Ops:
  7.2 0.0 all-gather.6.cloned.1.call-start
  7.2 1.7 copy.15
  8.9 0.0 all-gather.6.cloned.1.call-update
  8.9 0.0 reduce-scatter.2.cloned.1.call-start
  8.9 0.7 reshape.41
  9.6 24.7 %all-gather.2 = bf16[16,1,512]{2,1,0:T(2,128)(2,1)S(1)} all-gather(bf16[1,1,512]{2,1,0:T(2,128)(2,1)S(1)} %reshape.41), channel_id=1, replica_groups=mesh['pair'=2,'batch'=4,'vocab'=16] {'vocab'}, dimensions={0}, use_global_device_ids=true | all-gather | bytes 17408 | tf_op jit(solution)/shard_map/all_gather | solution.py:13
  34.4 24.1 %all-gather.6.cloned.1.call-done = bf16[1,128,8192]{1,2,0:T(8,128)(2,1)} async-done(((bf16[1,128,512]{1,2,0:T(8,128)(2,1)}), bf16[1,128,8192]{1,2,0:T(8,128)(2,1)}) %all-gather.6.cloned.1.call-update) | async-done | bytes 2097168 | tf_op jit(solution)/shard_map/all_gather | solution.py:12
  58.5 0.0 copy-start.1
  58.5 2.8 fusion
  61.3 0.0 copy-done.1
  61.3 3.5 %fusion.2 = bf16[128,8192]{0,1:T(8,128)(2,1)S(1)} fusion(bf16[1,128,8192]{1,2,0:T(8,128)(2,1)S(1)} %copy-done.1, f32[8192]{0:T(1024)S(1)} %bitcast.31, f32[128]{0:T(128)S(1)} %add_rsqrt_fusion), kind=kLoop, calls=%fused_computation.4 | loop fusion | flops 4194304 | bytes 4227584 | tf_op jit(solution)/shard_map/convert_element_type | solution.py:17
  64.8 30.7 %all_to_all.16 = bf16[128,8,1024]{0,2,1:T(8,128)(2,1)S(1)} all-to-all(bf16[128,8,1024]{0,2,1:T(8,128)(2,1)S(1)} %bitcast.27), channel_id=1, replica_groups=mesh['pair'=2,'batch'=4,'vocab'=16] {'pair','batch'}, dimensions={1} | all-to-all | bytes 4194304 | tf_op jit(solution)/shard_map/all_to_all | solution.py:18
  95.5 2.6 copy.16
  98.1 1.8 copy.17
  99.9 14.4 %fusion.6 = f32[1024,4096]{1,0:T(8,128)} fusion(bf16[1024,1024]{1,0:T(8,128)(2,1)S(1)} %bitcast.30, bf16[1024,4096]{1,0:T(8,128)(2,1)} %param.5), kind=kOutput, calls=%fused_computation.21 | convolution fusion | flops 8589934592 | bytes 27262976 | tf_op jit(solution)/shard_map/dot_general | solution.py:24
  114.3 0.0 reduce-scatter.2.cloned.1.call-update
  114.3 168.4 %reduce-scatter.2.cloned.1.call-done = f32[128,4096]{1,0:T(8,128)} async-done(((f32[1024,4096]{1,0:T(8,128)}), f32[128,4096]{1,0:T(8,128)}) %reduce-scatter.2.cloned.1.call-update) | async-done | bytes 2097168 | tf_op jit(solution)/shard_map/reduce_scatter | solution.py:23
  282.7 0.0 copy-start
  282.7 2.0 slice_reduce_fusion
  284.7 0.3 copy-done
  284.9 0.5 exponential_reduce_fusion.1
  285.5 23.5 %all-gather.3 = f32[16,4,64]{2,1,0:T(4,128)S(1)} all-gather(f32[1,4,64]{2,1,0:T(4,128)S(1)} %maximum_bitcast_fusion), channel_id=3, replica_groups=mesh['pair'=2,'batch'=4,'vocab'=16] {'vocab'}, dimensions={0}, use_global_device_ids=true | all-gather | bytes 17408 | tf_op jit(solution)/shard_map/all_gather | solution.py:37
  309.1 1.6 slice_subtract_fusion
  (8 shorter events, 0.2 us)
Async XLA Ops:
  7.2 51.3 %all-gather.6.cloned.1.call-start = ((), (), s32[]{:S(2)}) async-start(), calls=%async_computation.3 | async-start | bytes 2228224 | tf_op jit(solution)/shard_map/all_gather | solution.py:12
  8.9 273.8 %reduce-scatter.2.cloned.1.call-start = ((), (), s32[]{:S(2)}) async-start(), calls=%async_computation.2 | async-start | bytes 18874368 | tf_op jit(solution)/shard_map/reduce_scatter | solution.py:23
  58.5 2.8 copy-start.1
  282.7 2.2 copy-start
Sparse Core Ops, SparseCore 0:
  10.7 47.7 all-gather.5
  114.5 168.2 reduce-scatter.1
where the time goes:
time: 318 us
  waiting for transfers between devices  193 us (61%)
  blocking collectives  78.9 us (25%)
  matrix products  14.4 us (5%)
  between operations  14.1 us (4%)
  other arithmetic  10.6 us (3%)
  local copies, waits for them, and re-layouts  7.03 us (2%)
    reduce_scatter x1, waiting for transfers between devices, on_device(): lax.psum_scatter(jnp.dot(ordered, head_weight, preferred_element_type=jnp...  168 us
    all_to_all x1, blocking collectives, on_device(): lax.all_to_all(features, ('pair', 'batch'), split_axis=1, concat_axis=0,...  30.7 us
    all_gather x1, blocking collectives, on_device(): gain = lax.all_gather(norm_gain, 'vocab', axis=0, tiled=True)  24.7 us
    all_gather x1, waiting for transfers between devices, on_device(): rows = lax.all_gather(hidden[0], 'vocab', axis=1, tiled=True)  24.1 us
    all_gather x1, blocking collectives, on_device(): every = lax.all_gather(stats, 'vocab', axis=0)  23.5 us
    dot_general x1, matrix products, on_device(): jnp.dot(ordered, head_weight, preferred_element_type=jnp.float32)  14.4 us
  transfers between devices with their start and end apart: 2, of which 2 were waited for; matrix products, arithmetic and copies ran while one was open for 0% of the time, Pallas kernels for 0%

commit v1 on v0

--- a/solution.py
+++ b/solution.py
@@ -1,3 +1,4 @@
+import functools
 import jax
 import jax.numpy as jnp
 from jax import lax
@@ -8,8 +9,34 @@
 GUIDE = 1.5
 
 
+def track_plate(v0, device_axis):
+    block_next, later, u1 = (lax.axis_size(device_axis), lax.axis_index(device_axis), v0.shape[1])
+    vals = [(src_i, (src_i + 1) % block_next) for src_i in range(block_next)]
+    mixed_arr = jnp.zeros((*v0.shape[:1], block_next * u1, *v0.shape[2:]), v0.dtype)
+    mixed_arr = lax.dynamic_update_slice_in_dim(mixed_arr, v0, later * u1, axis=1)
+    everything = carry_in = v0
+    state_now = block_next // 2
+    u = 1
+    frames = [(src_i, (src_i - 1) % block_next) for src_i in range(block_next)]
+    while u < state_now + 1:
+        everything = lax.ppermute(everything, device_axis, perm=vals)
+        mixed_arr = lax.dynamic_update_slice_in_dim(
+            mixed_arr, everything, (later - u) % block_next * u1, axis=1
+        )
+        if u < block_next - state_now:
+            carry_in = lax.ppermute(carry_in, device_axis, frames)
+            mixed_arr = lax.dynamic_update_slice_in_dim(
+                mixed_arr, carry_in, (later + u) % block_next * u1, axis=1
+            )
+        u += 1
+    return mixed_arr
+
+
+obtain_copies = functools.partial(track_plate, device_axis="vocab")
+
+
 def on_device(hidden, norm_gain, head_weight):
-    rows = lax.all_gather(hidden[0], "vocab", axis=1, tiled=True)
+    rows = obtain_copies(hidden[0])
     gain = lax.all_gather(norm_gain, "vocab", axis=0, tiled=True)
     wide = rows.astype(jnp.float32)
     total_sq = jnp.sum(wide * wide, axis=1)

time: 318 us -> 351 us (1.10)
  starting transfers between devices: 0.08 us -> 40 us
    ppermute x0 -> x15, starting transfers between devices: none -> 40 us  [the longest x7 36.7 us: track_plate(): carry_in = lax.ppermute(carry_in, device_axis, frames)]
    ppermute x0 -> x15, waiting for transfers between devices: none -> 25.8 us  [the longest x8 25.8 us: track_plate(): everything = lax.ppermute(everything, device_axis, perm=vals)]
    all_gather x1 -> x0, waiting for transfers between devices: 24.1 us -> none  [on_device(): rows = lax.all_gather(hidden[0], 'vocab', axis=1, tiled=True)]
    all_gather x1, blocking collectives: 24.7 us -> 21.1 us  [on_device(): gain = lax.all_gather(norm_gain, 'vocab', axis=0, tiled=True)]
  transfers between devices with their start and end apart: 2 -> 16, of which waited for: 2 -> 8; matrix products, arithmetic and copies ran while one was open for 0% -> 0% of each run, Pallas kernels for 0% -> 0%
where the time goes in v1:
time: 351 us
  waiting for transfers between devices  191 us (54%)
  blocking collectives  75.4 us (21%)
  starting transfers between devices  40 us (11%)
  matrix products  14.4 us (4%)
  between operations  14.3 us (4%)
  other arithmetic  8.85 us (3%)
  local copies, waits for them, and re-layouts  6.99 us (2%)
    reduce_scatter x1, waiting for transfers between devices, on_device(): lax.psum_scatter(jnp.dot(ordered, head_weight, preferred_element_type=jnp...  165 us
    ppermute x7, starting transfers between devices, track_plate(): carry_in = lax.ppermute(carry_in, device_axis, frames)  36.7 us
    all_to_all x1, blocking collectives, on_device(): lax.all_to_all(features, ('pair', 'batch'), split_axis=1, concat_axis=0,...  30.8 us
    ppermute x8, waiting for transfers between devices, track_plate(): everything = lax.ppermute(everything, device_axis, perm=vals)  25.8 us
    all_gather x1, blocking collectives, on_device(): every = lax.all_gather(stats, 'vocab', axis=0)  23.5 us
    all_gather x1, blocking collectives, on_device(): gain = lax.all_gather(norm_gain, 'vocab', axis=0, tiled=True)  21.1 us
    dot_general x1, matrix products, on_device(): jnp.dot(ordered, head_weight, preferred_element_type=jnp.float32)  14.4 us
  transfers between devices with their start and end apart: 16, of which 8 were waited for; matrix products, arithmetic and copies ran while one was open for 0% of the time, Pallas kernels for 0%

profile of v1, /device:TPU:0, one launch (start us, length us, event | category | flops | bytes accessed | tf_op | source)
XLA Modules:
  0.0 351.2 jit_solution(10631374595467063336)
XLA Ops:
  7.2 0.0 reduce-scatter.2.cloned.1.call-start
  7.2 1.0 copy.15
  8.2 2.1 collective-permute-start
  10.3 4.4 %collective-permute-start.1 = (bf16[128,512]{0,1:T(8,128)(2,1)S(1)}, bf16[128,512]{0,1:T(8,128)(2,1)S(1)}, u32[]{:S(2)}, u32[]{:S(2)}) collective-permute-start(bf16[128,512]{0,1:T(8,128)(2,1)S(1)} %bitcast.30), channel_id=1, source_target_pairs={{0,15},{1,0},{2,1},{3,2},{4,3},{5,4},{6,5},{7,6},{8,7},{9,8},{10,9... | collective-permute-start | bytes 393224 | tf_op jit(solution)/shard_map/ppermute | solution.py:27
  14.7 0.7 reshape.39
  15.4 21.1 %all-gather.1 = bf16[16,1,512]{2,1,0:T(2,128)(2,1)S(1)} all-gather(bf16[1,1,512]{2,1,0:T(2,128)(2,1)S(1)} %reshape.39), channel_id=1, replica_groups=mesh['pair'=2,'batch'=4,'vocab'=16] {'vocab'}, dimensions={0}, use_global_device_ids=true | all-gather | bytes 17408 | tf_op jit(solution)/shard_map/all_gather | solution.py:40
  36.6 0.3 broadcast_in_dim.2
  36.9 0.0 collective-permute-done
  36.9 1.3 collective-permute-start.2
  38.2 0.0 collective-permute-done.1
  38.2 4.2 %collective-permute-start.3 = (bf16[128,512]{0,1:T(8,128)(2,1)S(1)}, bf16[128,512]{0,1:T(8,128)(2,1)S(1)}, u32[]{:S(2)}, u32[]{:S(2)}) collective-permute-start(bf16[128,512]{0,1:T(8,128)(2,1)S(1)} %collective-permute-done.1), channel_id=1, source_target_pairs={{0,15},{1,0},{2,1},{3,2},{4,3},{5,4},{6,5},{7,6},{8,7},{9,8},{10,9... | collective-permute-start | bytes 393224 | tf_op jit(solution)/shard_map/ppermute | solution.py:27
  42.4 4.0 %collective-permute-done.2 = bf16[128,512]{0,1:T(8,128)(2,1)S(1)} collective-permute-done((bf16[128,512]{0,1:T(8,128)(2,1)S(1)}, bf16[128,512]{0,1:T(8,128)(2,1)S(1)}, u32[]{:S(2)}, u32[]{:S(2)}) %collective-permute-start.2) | collective-permute-done | bytes 131104 | tf_op jit(solution)/shard_map/ppermute | solution.py:22
  46.4 0.0 collective-permute-start.4
  46.4 0.0 collective-permute-done.3
  46.4 5.6 %collective-permute-start.5 = (bf16[128,512]{0,1:T(8,128)(2,1)S(1)}, bf16[128,512]{0,1:T(8,128)(2,1)S(1)}, u32[]{:S(2)}, u32[]{:S(2)}) collective-permute-start(bf16[128,512]{0,1:T(8,128)(2,1)S(1)} %collective-permute-done.3), channel_id=1, source_target_pairs={{0,15},{1,0},{2,1},{3,2},{4,3},{5,4},{6,5},{7,6},{8,7},{9,8},{10,9... | collective-permute-start | bytes 393224 | tf_op jit(solution)/shard_map/ppermute | solution.py:27
  52.0 3.2 collective-permute-done.4
  55.2 0.0 collective-permute-start.6
  55.2 0.0 collective-permute-done.5
  55.2 5.6 %collective-permute-start.7 = (bf16[128,512]{0,1:T(8,128)(2,1)S(1)}, bf16[128,512]{0,1:T(8,128)(2,1)S(1)}, u32[]{:S(2)}, u32[]{:S(2)}) collective-permute-start(bf16[128,512]{0,1:T(8,128)(2,1)S(1)} %collective-permute-done.5), channel_id=1, source_target_pairs={{0,15},{1,0},{2,1},{3,2},{4,3},{5,4},{6,5},{7,6},{8,7},{9,8},{10,9... | collective-permute-start | bytes 393224 | tf_op jit(solution)/shard_map/ppermute | solution.py:27
  60.9 2.6 collective-permute-done.6
  63.5 0.0 collective-permute-start.8
  63.5 0.0 collective-permute-done.7
  63.5 5.6 %collective-permute-start.9 = (bf16[128,512]{0,1:T(8,128)(2,1)S(1)}, bf16[128,512]{0,1:T(8,128)(2,1)S(1)}, u32[]{:S(2)}, u32[]{:S(2)}) collective-permute-start(bf16[128,512]{0,1:T(8,128)(2,1)S(1)} %collective-permute-done.7), channel_id=1, source_target_pairs={{0,15},{1,0},{2,1},{3,2},{4,3},{5,4},{6,5},{7,6},{8,7},{9,8},{10,9... | collective-permute-start | bytes 393224 | tf_op jit(solution)/shard_map/ppermute | solution.py:27
  69.2 2.6 collective-permute-done.8
  71.8 0.0 collective-permute-start.10
  71.8 0.0 collective-permute-done.9
  71.8 5.6 %collective-permute-start.11 = (bf16[128,512]{0,1:T(8,128)(2,1)S(1)}, bf16[128,512]{0,1:T(8,128)(2,1)S(1)}, u32[]{:S(2)}, u32[]{:S(2)}) collective-permute-start(bf16[128,512]{0,1:T(8,128)(2,1)S(1)} %collective-permute-done.9), channel_id=1, source_target_pairs={{0,15},{1,0},{2,1},{3,2},{4,3},{5,4},{6,5},{7,6},{8,7},{9,8},{10,9... | collective-permute-start | bytes 393224 | tf_op jit(solution)/shard_map/ppermute | solution.py:27
  77.5 2.6 collective-permute-done.10
  80.1 0.0 collective-permute-start.12
  80.1 0.0 collective-permute-done.11
  80.1 5.6 %collective-permute-start.13 = (bf16[128,512]{0,1:T(8,128)(2,1)S(1)}, bf16[128,512]{0,1:T(8,128)(2,1)S(1)}, u32[]{:S(2)}, u32[]{:S(2)}) collective-permute-start(bf16[128,512]{0,1:T(8,128)(2,1)S(1)} %collective-permute-done.11), channel_id=1, source_target_pairs={{0,15},{1,0},{2,1},{3,2},{4,3},{5,4},{6,5},{7,6},{8,7},{9,8},{10,9... | collective-permute-start | bytes 393224 | tf_op jit(solution)/shard_map/ppermute | solution.py:27
  85.7 2.6 collective-permute-done.12
  88.4 0.0 collective-permute-start.14
  88.4 0.0 collective-permute-done.13
  88.4 8.2 %collective-permute-done.14 = bf16[128,512]{0,1:T(8,128)(2,1)S(1)} collective-permute-done((bf16[128,512]{0,1:T(8,128)(2,1)S(1)}, bf16[128,512]{0,1:T(8,128)(2,1)S(1)}, u32[]{:S(2)}, u32[]{:S(2)}) %collective-permute-start.14) | collective-permute-done | bytes 131104 | tf_op jit(solution)/shard_map/ppermute | solution.py:22
  96.7 1.1 fusion
  97.8 3.5 fusion.2
  101.2 30.8 %all_to_all.16 = bf16[128,8,1024]{0,2,1:T(8,128)(2,1)S(1)} all-to-all(bf16[128,8,1024]{0,2,1:T(8,128)(2,1)S(1)} %bitcast.25), channel_id=1, replica_groups=mesh['pair'=2,'batch'=4,'vocab'=16] {'pair','batch'}, dimensions={1} | all-to-all | bytes 4194304 | tf_op jit(solution)/shard_map/all_to_all | solution.py:45
  132.1 2.6 copy.16
  134.7 1.8 copy.17
  136.5 14.4 %fusion.6 = f32[1024,4096]{1,0:T(8,128)} fusion(bf16[1024,1024]{1,0:T(8,128)(2,1)S(1)} %bitcast.28, bf16[1024,4096]{1,0:T(8,128)(2,1)} %param.5), kind=kOutput, calls=%fused_computation.37 | convolution fusion | flops 8589934592 | bytes 27262976 | tf_op jit(solution)/shard_map/dot_general | solution.py:51
  150.9 0.0 reduce-scatter.2.cloned.1.call-update
  151.0 165.4 %reduce-scatter.2.cloned.1.call-done = f32[128,4096]{1,0:T(8,128)} async-done(((f32[1024,4096]{1,0:T(8,128)}), f32[128,4096]{1,0:T(8,128)}) %reduce-scatter.2.cloned.1.call-update) | async-done | bytes 2097168 | tf_op jit(solution)/shard_map/reduce_scatter | solution.py:50
  316.3 2.0 slice_reduce_fusion
  318.3 0.3 copy-done
  318.5 0.5 exponential_reduce_fusion.1
  319.1 23.5 %all-gather.2 = f32[16,4,64]{2,1,0:T(4,128)S(1)} all-gather(f32[1,4,64]{2,1,0:T(4,128)S(1)} %maximum_bitcast_fusion), channel_id=2, replica_groups=mesh['pair'=2,'batch'=4,'vocab'=16] {'vocab'}, dimensions={0}, use_global_device_ids=true | all-gather | bytes 17408 | tf_op jit(solution)/shard_map/all_gather | solution.py:64
  342.7 1.6 slice_subtract_fusion
  (25 shorter events, 0.5 us)
Async XLA Ops:
  7.2 309.2 %reduce-scatter.2.cloned.1.call-start = ((), (), s32[]{:S(2)}) async-start(), calls=%async_computation.2 | async-start | bytes 18874368 | tf_op jit(solution)/shard_map/reduce_scatter | solution.py:50
  8.2 28.6 %collective-permute-start = (bf16[128,512]{0,1:T(8,128)(2,1)S(1)}, bf16[128,512]{0,1:T(8,128)(2,1)S(1)}, u32[]{:S(2)}, u32[]{:S(2)}) collective-permute-start(bf16[128,512]{0,1:T(8,128)(2,1)S(1)} %bitcast.29), channel_id=1, source_target_pairs={{0,1},{1,2},{2,3},{3,4},{4,5},{5,6},{6,7},{7,8},{8,9},{9,10},{10,1... | collective-permute-start | bytes 393224 | tf_op jit(solution)/shard_map/ppermute | solution.py:22
  10.3 27.9 %collective-permute-start.1 = (bf16[128,512]{0,1:T(8,128)(2,1)S(1)}, bf16[128,512]{0,1:T(8,128)(2,1)S(1)}, u32[]{:S(2)}, u32[]{:S(2)}) collective-permute-start(bf16[128,512]{0,1:T(8,128)(2,1)S(1)} %bitcast.30), channel_id=1, source_target_pairs={{0,15},{1,0},{2,1},{3,2},{4,3},{5,4},{6,5},{7,6},{8,7},{9,8},{10,9... | collective-permute-start | bytes 393224 | tf_op jit(solution)/shard_map/ppermute | solution.py:27
  36.9 9.5 %collective-permute-start.2 = (bf16[128,512]{0,1:T(8,128)(2,1)S(1)}, bf16[128,512]{0,1:T(8,128)(2,1)S(1)}, u32[]{:S(2)}, u32[]{:S(2)}) collective-permute-start(bf16[128,512]{0,1:T(8,128)(2,1)S(1)} %collective-permute-done), channel_id=1, source_target_pairs={{0,1},{1,2},{2,3},{3,4},{4,5},{5,6},{6,7},{7,8},{8,9},{9,10},{10,1... | collective-permute-start | bytes 393224 | tf_op jit(solution)/shard_map/ppermute | solution.py:22
  38.2 8.2 %collective-permute-start.3 = (bf16[128,512]{0,1:T(8,128)(2,1)S(1)}, bf16[128,512]{0,1:T(8,128)(2,1)S(1)}, u32[]{:S(2)}, u32[]{:S(2)}) collective-permute-start(bf16[128,512]{0,1:T(8,128)(2,1)S(1)} %collective-permute-done.1), channel_id=1, source_target_pairs={{0,15},{1,0},{2,1},{3,2},{4,3},{5,4},{6,5},{7,6},{8,7},{9,8},{10,9... | collective-permute-start | bytes 393224 | tf_op jit(solution)/shard_map/ppermute | solution.py:27
  46.4 8.8 %collective-permute-start.4 = (bf16[128,512]{0,1:T(8,128)(2,1)S(1)}, bf16[128,512]{0,1:T(8,128)(2,1)S(1)}, u32[]{:S(2)}, u32[]{:S(2)}) collective-permute-start(bf16[128,512]{0,1:T(8,128)(2,1)S(1)} %collective-permute-done.2), channel_id=1, source_target_pairs={{0,1},{1,2},{2,3},{3,4},{4,5},{5,6},{6,7},{7,8},{8,9},{9,10},{10,1... | collective-permute-start | bytes 393224 | tf_op jit(solution)/shard_map/ppermute | solution.py:22
  46.4 8.8 %collective-permute-start.5 = (bf16[128,512]{0,1:T(8,128)(2,1)S(1)}, bf16[128,512]{0,1:T(8,128)(2,1)S(1)}, u32[]{:S(2)}, u32[]{:S(2)}) collective-permute-start(bf16[128,512]{0,1:T(8,128)(2,1)S(1)} %collective-permute-done.3), channel_id=1, source_target_pairs={{0,15},{1,0},{2,1},{3,2},{4,3},{5,4},{6,5},{7,6},{8,7},{9,8},{10,9... | collective-permute-start | bytes 393224 | tf_op jit(solution)/shard_map/ppermute | solution.py:27
  55.2 8.3 %collective-permute-start.6 = (bf16[128,512]{0,1:T(8,128)(2,1)S(1)}, bf16[128,512]{0,1:T(8,128)(2,1)S(1)}, u32[]{:S(2)}, u32[]{:S(2)}) collective-permute-start(bf16[128,512]{0,1:T(8,128)(2,1)S(1)} %collective-permute-done.4), channel_id=1, source_target_pairs={{0,1},{1,2},{2,3},{3,4},{4,5},{5,6},{6,7},{7,8},{8,9},{9,10},{10,1... | collective-permute-start | bytes 393224 | tf_op jit(solution)/shard_map/ppermute | solution.py:22
  55.2 8.3 %collective-permute-start.7 = (bf16[128,512]{0,1:T(8,128)(2,1)S(1)}, bf16[128,512]{0,1:T(8,128)(2,1)S(1)}, u32[]{:S(2)}, u32[]{:S(2)}) collective-permute-start(bf16[128,512]{0,1:T(8,128)(2,1)S(1)} %collective-permute-done.5), channel_id=1, source_target_pairs={{0,15},{1,0},{2,1},{3,2},{4,3},{5,4},{6,5},{7,6},{8,7},{9,8},{10,9... | collective-permute-start | bytes 393224 | tf_op jit(solution)/shard_map/ppermute | solution.py:27
  63.5 8.3 %collective-permute-start.8 = (bf16[128,512]{0,1:T(8,128)(2,1)S(1)}, bf16[128,512]{0,1:T(8,128)(2,1)S(1)}, u32[]{:S(2)}, u32[]{:S(2)}) collective-permute-start(bf16[128,512]{0,1:T(8,128)(2,1)S(1)} %collective-permute-done.6), channel_id=1, source_target_pairs={{0,1},{1,2},{2,3},{3,4},{4,5},{5,6},{6,7},{7,8},{8,9},{9,10},{10,1... | collective-permute-start | bytes 393224 | tf_op jit(solution)/shard_map/ppermute | solution.py:22
  63.5 8.3 %collective-permute-start.9 = (bf16[128,512]{0,1:T(8,128)(2,1)S(1)}, bf16[128,512]{0,1:T(8,128)(2,1)S(1)}, u32[]{:S(2)}, u32[]{:S(2)}) collective-permute-start(bf16[128,512]{0,1:T(8,128)(2,1)S(1)} %collective-permute-done.7), channel_id=1, source_target_pairs={{0,15},{1,0},{2,1},{3,2},{4,3},{5,4},{6,5},{7,6},{8,7},{9,8},{10,9... | collective-permute-start | bytes 393224 | tf_op jit(solution)/shard_map/ppermute | solution.py:27
  71.8 8.3 %collective-permute-start.10 = (bf16[128,512]{0,1:T(8,128)(2,1)S(1)}, bf16[128,512]{0,1:T(8,128)(2,1)S(1)}, u32[]{:S(2)}, u32[]{:S(2)}) collective-permute-start(bf16[128,512]{0,1:T(8,128)(2,1)S(1)} %collective-permute-done.8), channel_id=1, source_target_pairs={{0,1},{1,2},{2,3},{3,4},{4,5},{5,6},{6,7},{7,8},{8,9},{9,10},{10,1... | collective-permute-start | bytes 393224 | tf_op jit(solution)/shard_map/ppermute | solution.py:22
  71.8 8.3 %collective-permute-start.11 = (bf16[128,512]{0,1:T(8,128)(2,1)S(1)}, bf16[128,512]{0,1:T(8,128)(2,1)S(1)}, u32[]{:S(2)}, u32[]{:S(2)}) collective-permute-start(bf16[128,512]{0,1:T(8,128)(2,1)S(1)} %collective-permute-done.9), channel_id=1, source_target_pairs={{0,15},{1,0},{2,1},{3,2},{4,3},{5,4},{6,5},{7,6},{8,7},{9,8},{10,9... | collective-permute-start | bytes 393224 | tf_op jit(solution)/shard_map/ppermute | solution.py:27
  80.1 8.3 %collective-permute-start.12 = (bf16[128,512]{0,1:T(8,128)(2,1)S(1)}, bf16[128,512]{0,1:T(8,128)(2,1)S(1)}, u32[]{:S(2)}, u32[]{:S(2)}) collective-permute-start(bf16[128,512]{0,1:T(8,128)(2,1)S(1)} %collective-permute-done.10), channel_id=1, source_target_pairs={{0,1},{1,2},{2,3},{3,4},{4,5},{5,6},{6,7},{7,8},{8,9},{9,10},{10,1... | collective-permute-start | bytes 393224 | tf_op jit(solution)/shard_map/ppermute | solution.py:22
  80.1 8.3 %collective-permute-start.13 = (bf16[128,512]{0,1:T(8,128)(2,1)S(1)}, bf16[128,512]{0,1:T(8,128)(2,1)S(1)}, u32[]{:S(2)}, u32[]{:S(2)}) collective-permute-start(bf16[128,512]{0,1:T(8,128)(2,1)S(1)} %collective-permute-done.11), channel_id=1, source_target_pairs={{0,15},{1,0},{2,1},{3,2},{4,3},{5,4},{6,5},{7,6},{8,7},{9,8},{10,9... | collective-permute-start | bytes 393224 | tf_op jit(solution)/shard_map/ppermute | solution.py:27
  88.4 8.3 %collective-permute-start.14 = (bf16[128,512]{0,1:T(8,128)(2,1)S(1)}, bf16[128,512]{0,1:T(8,128)(2,1)S(1)}, u32[]{:S(2)}, u32[]{:S(2)}) collective-permute-start(bf16[128,512]{0,1:T(8,128)(2,1)S(1)} %collective-permute-done.12), channel_id=1, source_target_pairs={{0,1},{1,2},{2,3},{3,4},{4,5},{5,6},{6,7},{7,8},{8,9},{9,10},{10,1... | collective-permute-start | bytes 393224 | tf_op jit(solution)/shard_map/ppermute | solution.py:22
  316.3 2.2 copy-start
Sparse Core Ops, SparseCore 0:
  151.1 165.2 reduce-scatter.1
